TPU v7x, 32 devices: a whole 2x2x4 slice. The times are simulated.
32 devices in a mesh: space: 8 (over z, y), rep: 4 (over x, core).
Axes of the slice: x: 2, y: 2, z: 4, core: 2. Of those that a mesh axis runs over, the one named last changes fastest.
Arguments:
- volumes: bfloat16 [4, 8, 8, 4, 16, 256], P('rep', 'space'), may hold values from -6 to 6
- grad_parts: bfloat16 [4, 2, 6912, 256], P('rep', None, 'space'), may hold values from -6 to 6
- master_weights: float32 [2, 6912, 256], P(None, 'space'), may hold values from -0.078125 to 0.078125
- moment_first: float32 [4, 2, 6912, 256], P('rep', None, 'space'), may hold values from -12 to 12
- moment_second: float32 [4, 2, 6912, 256], P('rep', None, 'space'), may hold values from 1 to 30
- owner: int32 [2, 32], replicated, may hold values from 0 to 3
Outputs:
- features: bfloat16 [4, 8, 8, 4, 16, 256], P('rep', 'space')
- new_weights: float32 [2, 1769472], P(None, ('space', 'rep'))
- moment_first_out: float32 [4, 2, 6912, 256], P('rep', None, 'space')
- moment_second_out: float32 [4, 2, 6912, 256], P('rep', None, 'space')
Inputs may be any that keep to these rules, and one draw needn't show every extreme that they name: owner[f, p] is the replica whose state slot holds the optimizer state of panel p of filter f, rows p * 216 to (p + 1) * 216 - 1; replicas may own unequal numbers of panels.
All inputs are finite; a program needn't handle non-finite values.
Results may differ from a plain program's by a relative error of at most 0.0095.
Values may be sent and summed in bfloat16 or wider, within the bound.
No kernel may reach another device: no remote copies, remote signals or barrier semaphores. Data moves between devices by JAX's collectives and lax.ppermute only.
A program may use at most 64 MiB of HBM per device.

v0:
```python
import jax
import jax.numpy as jnp
from jax import lax
from jax.sharding import PartitionSpec as P

GY = 2
GZ = 2
PANEL_ROWS = 216


def passed_along(value, axis, steps):
    count = lax.axis_size(axis)
    first, last = (max(0, -steps), min(count, count - steps))
    return lax.ppermute(value, axis, [(source, source + steps) for source in range(first, last)])


def spread(value, axis, source):
    kept = jnp.where(lax.axis_index(axis) == source, value, 0).astype(value.dtype)
    return lax.psum(kept, axis)


def neighbour(slab, offset):
    return passed_along(slab, "space", offset)


def keep_when(flag, slab):
    return jnp.where(flag, slab, jnp.zeros_like(slab))


def side_slab(array, dim, side):
    length = array.shape[dim]
    if side < 0:
        return lax.slice_in_dim(array, length - 1, length, 1, dim)
    return lax.slice_in_dim(array, 0, 1, 1, dim)


def extend_brick(brick, coords, strides, grid):
    lows = [coords[d] > 0 for d in range(3)]
    highs = [coords[d] < grid[d] - 1 for d in range(3)]
    current = brick
    for dim in range(3):
        lower = keep_when(lows[dim], neighbour(side_slab(current, dim, -1), strides[dim]))
        upper = keep_when(highs[dim], neighbour(side_slab(current, dim, 1), -strides[dim]))
        current = jnp.concatenate([lower, current, upper], axis=dim)
    return current


def convolve(extended, filter_rows):
    extent_x = extended.shape[0] - 2
    extent_y = extended.shape[1] - 2
    extent_z = extended.shape[2] - 2
    channels = extended.shape[3]
    summed = jnp.zeros((extent_x * extent_y * extent_z, filter_rows.shape[1]), jnp.float32)
    for shift_x in range(3):
        for shift_y in range(3):
            for shift_z in range(3):
                tap_index = (shift_x * 3 + shift_y) * 3 + shift_z
                window = extended[
                    shift_x : shift_x + extent_x,
                    shift_y : shift_y + extent_y,
                    shift_z : shift_z + extent_z,
                ]
                weights_tap = filter_rows[tap_index * channels : (tap_index + 1) * channels]
                summed = summed + jnp.dot(
                    window.reshape(-1, channels), weights_tap, preferred_element_type=jnp.float32
                )
    return summed.reshape(extent_x, extent_y, extent_z, -1)


def shards(volumes, grad_parts, master_weights, moment_first, moment_second, owner):
    filter_count = master_weights.shape[0]
    rows_dev = master_weights.shape[1]
    channels = master_weights.shape[2]
    panels_dev = rows_dev // PANEL_ROWS
    space_pos = lax.axis_index("space")
    rep_pos = lax.axis_index("rep")
    summed_grad = lax.psum(grad_parts[0].astype(jnp.float32).astype(jnp.bfloat16), "rep").astype(
        jnp.float32
    )
    first_new = 0.9 * moment_first[0] + 0.1 * summed_grad
    second_new = 0.95 * moment_second[0] + 0.05 * (summed_grad * summed_grad)
    owner_local = lax.dynamic_slice_in_dim(owner, space_pos * panels_dev, panels_dev, 1)
    owner_rows = jnp.repeat(owner_local, PANEL_ROWS, axis=1)
    owned = (owner_rows == rep_pos)[:, :, None]
    first_out = jnp.where(owned, first_new, moment_first[0])[None]
    second_out = jnp.where(owned, second_new, moment_second[0])[None]
    corr_one = 1.0 - 0.9**10
    corr_two = 1.0 - 0.95**10
    update = first_new / corr_one / (jnp.sqrt(second_new / corr_two) + 1e-08) + 0.1 * master_weights
    candidate = master_weights - 0.004 * update
    per_filter = []
    for filter_index in range(filter_count):
        slabs = []
        for panel_index in range(panels_dev):
            slab = candidate[
                filter_index, panel_index * PANEL_ROWS : (panel_index + 1) * PANEL_ROWS
            ]
            slabs.append(
                spread(
                    slab.astype(jnp.bfloat16), "rep", owner_local[filter_index, panel_index]
                ).astype(slab.dtype)
            )
        per_filter.append(jnp.concatenate(slabs, axis=0))
    new_master = jnp.stack(per_filter)
    share_len = rows_dev * channels // lax.axis_size("rep")
    new_weights = lax.dynamic_slice_in_dim(
        new_master.reshape(filter_count, -1), rep_pos * share_len, share_len, 1
    )
    filters = lax.all_gather(new_master.astype(jnp.bfloat16), "space", axis=1, tiled=True)
    grid = (lax.axis_size("space") // (GY * GZ), GY, GZ)
    strides = (GY * GZ, GZ, 1)
    coords = (space_pos // (GY * GZ), space_pos // GZ % GY, space_pos % GZ)
    brick = volumes[0, 0]
    hidden = jax.nn.gelu(
        convolve(extend_brick(brick, coords, strides, grid), filters[0]), approximate=True
    ).astype(jnp.bfloat16)
    output = jax.nn.gelu(
        convolve(extend_brick(hidden, coords, strides, grid), filters[1]), approximate=True
    ).astype(jnp.bfloat16)
    return (output[None, None], new_weights, first_out, second_out)


def solution(mesh):
    placed = (
        P("rep", "space", None, None, None, None),
        P("rep", None, "space", None),
        P(None, "space", None),
        P("rep", None, "space", None),
        P("rep", None, "space", None),
        P(),
    )
    return jax.shard_map(
        shards,
        mesh=mesh,
        in_specs=placed,
        out_specs=(
            P("rep", "space", None, None, None, None),
            P(None, ("space", "rep")),
            P("rep", None, "space", None),
            P("rep", None, "space", None),
        ),
        check_vma=False,
    )
```

profile of v0, /device:TPU:0, one launch (start us, length us, event | category | flops | bytes accessed | tf_op | source)
XLA Modules:
  0.0 271.1 jit_solution(5235828879841279045)
XLA Ops:
  14.8 34.0 %all-reduce.4.cloned.1.call-done = bf16[2,864,256]{2,1,0:T(8,128)(2,1)} async-done(((bf16[2,864,256]{2,1,0:T(8,128)(2,1)}), bf16[2,864,256]{2,1,0:T(8,128)(2,1)}) %all-reduce.4.cloned.1.call-update) | async-done | bytes 884752 | tf_op jit(solution)/shard_map/psum | solution.py:77
  48.7 4.8 %fusion.8 = (f32[1,2,864,256]{3,2,1,0:T(8,128)}, bf16[2,864,256]{2,1,0:T(8,128)(2,1)S(1)}, f32[1,2,864,256]{3,2,1,0:T(8,128)}) fusion(bf16[2,864,256]{2,1,0:T(8,128)(2,1)} %all-reduce.4.cloned.1.call-done, f32[1,2,864,256]{3,2,1,0:T(8,128)} %param.10, pred[2,864]{1,0:T(4,128)(4,1)S(1)} %eq.51, f32[2,864,256]{2,1,0:T(8,128)} %param.8, f32[1,2,864,256]{3,2,1,0:T(8,128)} %param.9), kind=kLoop, calls=%fused_computation.12 | loop fusion | flops 8404992 | bytes 10618560 | tf_op jit(solution)/shard_map/broadcast_in_dim | solution.py:86
  54.5 36.1 %all-reduce.6.cloned.1.call-done = (bf16[216,256]{1,0:T(8,128)(2,1)}, bf16[216,256]{1,0:T(8,128)(2,1)}, bf16[216,256]{1,0:T(8,128)(2,1)}, bf16[216,256]{1,0:T(8,...) async-done(((bf16[216,256]{1,0:T(8,128)(2,1)}, bf16[216,256]{1,0:T(8,128)(2,1)}, ...) | async-done | bytes 884752 | tf_op jit(solution)/shard_map/psum | solution.py:19
  98.1 4.3 %collective-permute-start = (bf16[1,4,16,256]{3,2,1,0:T(8,128)(2,1)S(1)}, bf16[1,4,16,256]{3,2,1,0:T(8,128)(2,1)S(1)}, u32[]{:S(2)}, u32[]{:S(2)}) collective-permute-start(bf16[1,4,16,256]{3,2,1,0:T(8,128)(2,1)S(1)} %get-tuple-element.95), channel_id=1, source_target_pairs={{0,16},{4,20},{8,24},{12,28},{1,17},{5,21},{9,25},{13,29},{2,18},{... | collective-permute-start | bytes 98312 | tf_op jit(solution)/shard_map/ppermute | solution.py:14
  104.0 5.1 %collective-permute-done.1 = bf16[1,4,16,256]{3,2,1,0:T(8,128)(2,1)S(1)} collective-permute-done((bf16[1,4,16,256]{3,2,1,0:T(8,128)(2,1)S(1)}, bf16[1,4,16,256]{3,2,1,0:T(8,128)(2,1)S(1)}, u32[]{:S(2)}, u32[]{:S(2)}) %collective-permute-start.1) | collective-permute-done | bytes 32800 | tf_op jit(solution)/shard_map/ppermute | solution.py:14
  109.2 3.4 %collective-permute-start.2 = (bf16[10,1,16,256]{3,2,1,0:T(8,128)(2,1)S(1)}, bf16[10,1,16,256]{3,2,1,0:T(8,128)(2,1)S(1)}, u32[]{:S(2)}, u32[]{:S(2)}) collective-permute-start(bf16[10,1,16,256]{3,2,1,0:T(8,128)(2,1)S(1)} %get-tuple-element.87), channel_id=1, source_target_pairs={{0,8},{4,12},{8,16},{12,20},{16,24},{20,28},{1,9},{5,13},{9,17},{1... | collective-permute-start | bytes 245768 | tf_op jit(solution)/shard_map/ppermute | solution.py:14
  112.6 1.3 collective-permute-start.3
  114.7 1.7 collective-permute-done.2
  116.4 6.2 %collective-permute-done.3 = bf16[10,1,16,256]{3,2,1,0:T(8,128)(2,1)S(1)} collective-permute-done((bf16[10,1,16,256]{3,2,1,0:T(8,128)(2,1)S(1)}, bf16[10,1,16,256]{3,2,1,0:T(8,128)(2,1)S(1)}, u32[]{:S(2)}, u32[]{:S(2)}) %collective-permute-start.3) | collective-permute-done | bytes 81952 | tf_op jit(solution)/shard_map/ppermute | solution.py:14
  122.7 3.4 %collective-permute-start.4 = (bf16[10,6,1,256]{3,2,1,0:T(2,128)(2,1)S(1)}, bf16[10,6,1,256]{3,2,1,0:T(2,128)(2,1)S(1)}, u32[]{:S(2)}, u32[]{:S(2)}) collective-permute-start(bf16[10,6,1,256]{3,2,1,0:T(2,128)(2,1)S(1)} %get-tuple-element.68), channel_id=1, source_target_pairs={{0,4},{4,8},{8,12},{12,16},{16,20},{20,24},{24,28},{1,5},{5,9},{9,... | collective-permute-start | bytes 92168 | tf_op jit(solution)/shard_map/ppermute | solution.py:14
  126.1 1.3 collective-permute-start.5
  128.7 3.5 %collective-permute-done.5 = bf16[10,6,1,256]{3,2,1,0:T(2,128)(2,1)S(1)} collective-permute-done((bf16[10,6,1,256]{3,2,1,0:T(2,128)(2,1)S(1)}, bf16[10,6,1,256]{3,2,1,0:T(2,128)(2,1)S(1)}, u32[]{:S(2)}, u32[]{:S(2)}) %collective-permute-start.5) | collective-permute-done | bytes 30752 | tf_op jit(solution)/shard_map/ppermute | solution.py:14
  132.8 2.2 fusion.75
  136.3 73.2 %all-gather.2.cloned.1.call-done = bf16[2,6912,256]{2,1,0:T(8,128)(2,1)} async-done(((bf16[2,864,256]{2,1,0:T(8,128)(2,1)}), bf16[2,6912,256]{2,1,0:T(8,128)(2,1)}) %all-gather.2.cloned.1.call-update) | async-done | bytes 7077904 | tf_op jit(solution)/shard_map/all_gather | solution.py:109
  209.6 1.4 fusion.60
  210.9 1.8 fusion.59
  226.9 3.4 %collective-permute-start.6 = (bf16[1,4,16,256]{3,2,1,0:T(8,128)(2,1)S(1)}, bf16[1,4,16,256]{3,2,1,0:T(8,128)(2,1)S(1)}, u32[]{:S(2)}, u32[]{:S(2)}) collective-permute-start(bf16[1,4,16,256]{3,2,1,0:T(8,128)(2,1)S(1)} %get-tuple-element.91), channel_id=1, source_target_pairs={{0,16},{4,20},{8,24},{12,28},{1,17},{5,21},{9,25},{13,29},{2,18},{... | collective-permute-start | bytes 98312 | tf_op jit(solution)/shard_map/ppermute | solution.py:14
  230.3 1.3 fusion.50
  232.9 5.7 %collective-permute-done.7 = bf16[1,4,16,256]{3,2,1,0:T(8,128)(2,1)S(1)} collective-permute-done((bf16[1,4,16,256]{3,2,1,0:T(8,128)(2,1)S(1)}, bf16[1,4,16,256]{3,2,1,0:T(8,128)(2,1)S(1)}, u32[]{:S(2)}, u32[]{:S(2)}) %collective-permute-start.7) | collective-permute-done | bytes 32800 | tf_op jit(solution)/shard_map/ppermute | solution.py:14
  238.6 2.1 collective-permute-start.8
  242.8 4.3 %collective-permute-done.9 = bf16[10,1,16,256]{3,2,1,0:T(8,128)(2,1)S(1)} collective-permute-done((bf16[10,1,16,256]{3,2,1,0:T(8,128)(2,1)S(1)}, bf16[10,1,16,256]{3,2,1,0:T(8,128)(2,1)S(1)}, u32[]{:S(2)}, u32[]{:S(2)}) %collective-permute-start.9) | collective-permute-done | bytes 81952 | tf_op jit(solution)/shard_map/ppermute | solution.py:14
  247.4 2.6 collective-permute-start.10
  250.0 1.5 collective-permute-start.11
  252.4 3.7 %collective-permute-done.11 = bf16[10,6,1,256]{3,2,1,0:T(2,128)(2,1)S(1)} collective-permute-done((bf16[10,6,1,256]{3,2,1,0:T(2,128)(2,1)S(1)}, bf16[10,6,1,256]{3,2,1,0:T(2,128)(2,1)S(1)}, u32[]{:S(2)}, u32[]{:S(2)}) %collective-permute-start.11) | collective-permute-done | bytes 30752 | tf_op jit(solution)/shard_map/ppermute | solution.py:14
  (146 shorter events, 43.2 us)
Async XLA Ops:
  7.2 41.6 %all-reduce.4.cloned.1.call-start = ((), (), s32[]{:S(2)}) async-start(), calls=%async_computation | async-start | bytes 1769472 | tf_op jit(solution)/shard_map/psum | solution.py:77
  7.9 82.7 %all-reduce.6.cloned.1.call-start = ((), (), s32[]{:S(2)}) async-start(), calls=%async_computation.2 | async-start | bytes 1769472 | tf_op jit(solution)/shard_map/psum | solution.py:19
  14.7 83.4 %copy-start = (bf16[1,1,8,4,16,256]{5,4,3,2,1,0:T(8,128)(2,1)S(1)}, bf16[1,1,8,4,16,256]{5,4,3,2,1,0:T(8,128)(2,1)}, u32[]{:S(2)}) copy-start(bf16[1,1,8,4,16,256]{5,4,3,2,1,0:T(8,128)(2,1)} %param.6) | copy-start | bytes 786436
  54.5 155.1 %all-gather.2.cloned.1.call-start = ((), (), s32[]{:S(2)}) async-start(), calls=%async_computation.1 | async-start | bytes 7962624 | tf_op jit(solution)/shard_map/all_gather | solution.py:109
  98.1 5.9 %collective-permute-start = (bf16[1,4,16,256]{3,2,1,0:T(8,128)(2,1)S(1)}, bf16[1,4,16,256]{3,2,1,0:T(8,128)(2,1)S(1)}, u32[]{:S(2)}, u32[]{:S(2)}) collective-permute-start(bf16[1,4,16,256]{3,2,1,0:T(8,128)(2,1)S(1)} %get-tuple-element.95), channel_id=1, source_target_pairs={{0,16},{4,20},{8,24},{12,28},{1,17},{5,21},{9,25},{13,29},{2,18},{... | collective-permute-start | bytes 98312 | tf_op jit(solution)/shard_map/ppermute | solution.py:14
  102.4 6.7 %collective-permute-start.1 = (bf16[1,4,16,256]{3,2,1,0:T(8,128)(2,1)S(1)}, bf16[1,4,16,256]{3,2,1,0:T(8,128)(2,1)S(1)}, u32[]{:S(2)}, u32[]{:S(2)}) collective-permute-start(bf16[1,4,16,256]{3,2,1,0:T(8,128)(2,1)S(1)} %get-tuple-element.96), channel_id=1, source_target_pairs={{16,0},{20,4},{24,8},{28,12},{17,1},{21,5},{25,9},{29,13},{18,2},{... | collective-permute-start | bytes 98312 | tf_op jit(solution)/shard_map/ppermute | solution.py:14
  109.2 7.2 %collective-permute-start.2 = (bf16[10,1,16,256]{3,2,1,0:T(8,128)(2,1)S(1)}, bf16[10,1,16,256]{3,2,1,0:T(8,128)(2,1)S(1)}, u32[]{:S(2)}, u32[]{:S(2)}) collective-permute-start(bf16[10,1,16,256]{3,2,1,0:T(8,128)(2,1)S(1)} %get-tuple-element.87), channel_id=1, source_target_pairs={{0,8},{4,12},{8,16},{12,20},{16,24},{20,28},{1,9},{5,13},{9,17},{1... | collective-permute-start | bytes 245768 | tf_op jit(solution)/shard_map/ppermute | solution.py:14
  112.6 10.0 %collective-permute-start.3 = (bf16[10,1,16,256]{3,2,1,0:T(8,128)(2,1)S(1)}, bf16[10,1,16,256]{3,2,1,0:T(8,128)(2,1)S(1)}, u32[]{:S(2)}, u32[]{:S(2)}) collective-permute-start(bf16[10,1,16,256]{3,2,1,0:T(8,128)(2,1)S(1)} %get-tuple-element.88), channel_id=1, source_target_pairs={{8,0},{12,4},{16,8},{20,12},{24,16},{28,20},{9,1},{13,5},{17,9},{2... | collective-permute-start | bytes 245768 | tf_op jit(solution)/shard_map/ppermute | solution.py:14
  122.7 5.9 %collective-permute-start.4 = (bf16[10,6,1,256]{3,2,1,0:T(2,128)(2,1)S(1)}, bf16[10,6,1,256]{3,2,1,0:T(2,128)(2,1)S(1)}, u32[]{:S(2)}, u32[]{:S(2)}) collective-permute-start(bf16[10,6,1,256]{3,2,1,0:T(2,128)(2,1)S(1)} %get-tuple-element.68), channel_id=1, source_target_pairs={{0,4},{4,8},{8,12},{12,16},{16,20},{20,24},{24,28},{1,5},{5,9},{9,... | collective-permute-start | bytes 92168 | tf_op jit(solution)/shard_map/ppermute | solution.py:14
  126.1 6.1 %collective-permute-start.5 = (bf16[10,6,1,256]{3,2,1,0:T(2,128)(2,1)S(1)}, bf16[10,6,1,256]{3,2,1,0:T(2,128)(2,1)S(1)}, u32[]{:S(2)}, u32[]{:S(2)}) collective-permute-start(bf16[10,6,1,256]{3,2,1,0:T(2,128)(2,1)S(1)} %get-tuple-element.67), channel_id=1, source_target_pairs={{4,0},{8,4},{12,8},{16,12},{20,16},{24,20},{28,24},{5,1},{9,5},{13... | collective-permute-start | bytes 92168 | tf_op jit(solution)/shard_map/ppermute | solution.py:14
  209.5 10.4 %copy-start.1 = (bf16[2,6912,256]{2,1,0:T(8,128)(2,1)S(1)}, bf16[2,6912,256]{2,1,0:T(8,128)(2,1)}, u32[]{:S(2)}) copy-start(bf16[2,6912,256]{2,1,0:T(8,128)(2,1)} %all-gather.2.cloned.1.call-done) | copy-start | bytes 21233668
  209.5 11.8 %copy-start.15 = (bf16[8,4,16,256]{3,2,1,0:T(8,128)(2,1)S(1)}, bf16[8,4,16,256]{3,2,1,0:T(8,128)(2,1)}, u32[]{:S(2)}) copy-start(bf16[8,4,16,256]{3,2,1,0:T(8,128)(2,1)} %get-tuple-element.51) | copy-start | bytes 786436
  209.6 12.1 %copy-start.14 = (bf16[8,4,16,256]{3,2,1,0:T(8,128)(2,1)S(1)}, bf16[8,4,16,256]{3,2,1,0:T(8,128)(2,1)}, u32[]{:S(2)}) copy-start(bf16[8,4,16,256]{3,2,1,0:T(8,128)(2,1)} %get-tuple-element.106) | copy-start | bytes 786436
  209.6 13.5 %copy-start.13 = (bf16[8,4,16,256]{3,2,1,0:T(8,128)(2,1)S(1)}, bf16[8,4,16,256]{3,2,1,0:T(8,128)(2,1)}, u32[]{:S(2)}) copy-start(bf16[8,4,16,256]{3,2,1,0:T(8,128)(2,1)} %get-tuple-element.50) | copy-start | bytes 786436
  210.9 12.4 %copy-start.12 = (bf16[8,4,16,256]{3,2,1,0:T(8,128)(2,1)S(1)}, bf16[8,4,16,256]{3,2,1,0:T(8,128)(2,1)}, u32[]{:S(2)}) copy-start(bf16[8,4,16,256]{3,2,1,0:T(8,128)(2,1)} %get-tuple-element.107) | copy-start | bytes 786436
  213.9 9.6 %copy-start.4 = (bf16[8,4,16,256]{3,2,1,0:T(8,128)(2,1)S(1)}, bf16[8,4,16,256]{3,2,1,0:T(8,128)(2,1)}, u32[]{:S(2)}) copy-start(bf16[8,4,16,256]{3,2,1,0:T(8,128)(2,1)} %get-tuple-element.77) | copy-start | bytes 786436
  216.3 7.5 %copy-start.11 = (bf16[8,4,16,256]{3,2,1,0:T(8,128)(2,1)S(1)}, bf16[8,4,16,256]{3,2,1,0:T(8,128)(2,1)}, u32[]{:S(2)}) copy-start(bf16[8,4,16,256]{3,2,1,0:T(8,128)(2,1)} %get-tuple-element.49) | copy-start | bytes 786436
  217.6 6.5 %copy-start.10 = (bf16[8,4,16,256]{3,2,1,0:T(8,128)(2,1)S(1)}, bf16[8,4,16,256]{3,2,1,0:T(8,128)(2,1)}, u32[]{:S(2)}) copy-start(bf16[8,4,16,256]{3,2,1,0:T(8,128)(2,1)} %get-tuple-element.108) | copy-start | bytes 786436
  226.9 6.0 %collective-permute-start.6 = (bf16[1,4,16,256]{3,2,1,0:T(8,128)(2,1)S(1)}, bf16[1,4,16,256]{3,2,1,0:T(8,128)(2,1)S(1)}, u32[]{:S(2)}, u32[]{:S(2)}) collective-permute-start(bf16[1,4,16,256]{3,2,1,0:T(8,128)(2,1)S(1)} %get-tuple-element.91), channel_id=1, source_target_pairs={{0,16},{4,20},{8,24},{12,28},{1,17},{5,21},{9,25},{13,29},{2,18},{... | collective-permute-start | bytes 98312 | tf_op jit(solution)/shard_map/ppermute | solution.py:14
  231.6 7.0 %collective-permute-start.7 = (bf16[1,4,16,256]{3,2,1,0:T(8,128)(2,1)S(1)}, bf16[1,4,16,256]{3,2,1,0:T(8,128)(2,1)S(1)}, u32[]{:S(2)}, u32[]{:S(2)}) collective-permute-start(bf16[1,4,16,256]{3,2,1,0:T(8,128)(2,1)S(1)} %get-tuple-element.92), channel_id=1, source_target_pairs={{16,0},{20,4},{24,8},{28,12},{17,1},{21,5},{25,9},{29,13},{18,2},{... | collective-permute-start | bytes 98312 | tf_op jit(solution)/shard_map/ppermute | solution.py:14
  238.6 4.2 %collective-permute-start.8 = (bf16[10,1,16,256]{3,2,1,0:T(8,128)(2,1)S(1)}, bf16[10,1,16,256]{3,2,1,0:T(8,128)(2,1)S(1)}, u32[]{:S(2)}, u32[]{:S(2)}) collective-permute-start(bf16[10,1,16,256]{3,2,1,0:T(8,128)(2,1)S(1)} %get-tuple-element.83), channel_id=1, source_target_pairs={{0,8},{4,12},{8,16},{12,20},{16,24},{20,28},{1,9},{5,13},{9,17},{1... | collective-permute-start | bytes 245768 | tf_op jit(solution)/shard_map/ppermute | solution.py:14
  240.8 6.3 %collective-permute-start.9 = (bf16[10,1,16,256]{3,2,1,0:T(8,128)(2,1)S(1)}, bf16[10,1,16,256]{3,2,1,0:T(8,128)(2,1)S(1)}, u32[]{:S(2)}, u32[]{:S(2)}) collective-permute-start(bf16[10,1,16,256]{3,2,1,0:T(8,128)(2,1)S(1)} %get-tuple-element.84), channel_id=1, source_target_pairs={{8,0},{12,4},{16,8},{20,12},{24,16},{28,20},{9,1},{13,5},{17,9},{2... | collective-permute-start | bytes 245768 | tf_op jit(solution)/shard_map/ppermute | solution.py:14
  247.4 4.9 %collective-permute-start.10 = (bf16[10,6,1,256]{3,2,1,0:T(2,128)(2,1)S(1)}, bf16[10,6,1,256]{3,2,1,0:T(2,128)(2,1)S(1)}, u32[]{:S(2)}, u32[]{:S(2)}) collective-permute-start(bf16[10,6,1,256]{3,2,1,0:T(2,128)(2,1)S(1)} %get-tuple-element.64), channel_id=1, source_target_pairs={{0,4},{4,8},{8,12},{12,16},{16,20},{20,24},{24,28},{1,5},{5,9},{9,... | collective-permute-start | bytes 92168 | tf_op jit(solution)/shard_map/ppermute | solution.py:14
  250.0 6.1 %collective-permute-start.11 = (bf16[10,6,1,256]{3,2,1,0:T(2,128)(2,1)S(1)}, bf16[10,6,1,256]{3,2,1,0:T(2,128)(2,1)S(1)}, u32[]{:S(2)}, u32[]{:S(2)}) collective-permute-start(bf16[10,6,1,256]{3,2,1,0:T(2,128)(2,1)S(1)} %get-tuple-element.63), channel_id=1, source_target_pairs={{4,0},{8,4},{12,8},{16,12},{20,16},{24,20},{28,24},{5,1},{9,5},{13... | collective-permute-start | bytes 92168 | tf_op jit(solution)/shard_map/ppermute | solution.py:14
  (8 other events, 21.5 us)
Sparse Core Ops, SparseCore 0:
  10.3 38.3 all-reduce.3
  54.6 35.9 all-reduce.5
  98.2 111.2 all-gather.1
where the time goes:
time: 272 us; the launch traced here: 271 us
  waiting for transfers between devices  176 us (65%)
  starting transfers between devices  27.3 us (10%)
  matrix products  22.9 us (8%)
  between operations  19.8 us (7%)
  local copies, waits for them, and re-layouts  12.8 us (5%)
  other arithmetic  12.4 us (5%)
    all_gather x1, waiting for transfers between devices, shards(): lax.all_gather(new_master.astype(jnp.bfloat16), 'space', axis=1, tiled=True)  73.2 us
    psum x1, waiting for transfers between devices, spread(): return lax.psum(kept, axis)  36.1 us
    psum x1, waiting for transfers between devices, shards(): lax.psum(grad_parts[0].astype(jnp.float32).astype(jnp.bfloat16), 'rep')  34 us
    ppermute x12, waiting for transfers between devices, passed_along(): lax.ppermute(value, axis, [(source, source + steps) for source in range(f...  31.9 us
    ppermute x12, starting transfers between devices, passed_along(): lax.ppermute(value, axis, [(source, source + steps) for source in range(f...  27.2 us
    dot_general x54, matrix products, convolve(): jnp.dot(window.reshape(-1, channels), weights_tap, preferred_element_type...  22.9 us
    unnamed x42, local copies, waits for them, and re-layouts  6.87 us
  transfers between devices with their start and end apart: 15, of which 13 were waited for; matrix products, arithmetic and copies ran while one was open for 3% of the time, Pallas kernels for 0%

commit v1 on v0

--- a/solution.py
+++ b/solution.py
@@ -2,10 +2,23 @@
 import jax.numpy as jnp
 from jax import lax
 from jax.sharding import PartitionSpec as P
+from jax.lax import axis_index, axis_size, ppermute
 
 GY = 2
 GZ = 2
 PANEL_ROWS = 216
+
+
+def boxes_supply_all(load):
+    bank = [load]
+    n_parts = axis_size("space")
+    j0 = 1
+    while j0 < n_parts:
+        now = ppermute(bank[j0 - 1], "space", [(i0, (i0 - 1) % n_parts) for i0 in range(n_parts)])
+        bank.append(now)
+        j0 += 1
+    main = jnp.concatenate(bank, 1)
+    return jnp.roll(main, shift=axis_index("space") * load.shape[1], axis=1)
 
 
 def passed_along(value, axis, steps):
@@ -106,7 +119,7 @@
     new_weights = lax.dynamic_slice_in_dim(
         new_master.reshape(filter_count, -1), rep_pos * share_len, share_len, 1
     )
-    filters = lax.all_gather(new_master.astype(jnp.bfloat16), "space", axis=1, tiled=True)
+    filters = boxes_supply_all(new_master.astype(jnp.bfloat16))
     grid = (lax.axis_size("space") // (GY * GZ), GY, GZ)
     strides = (GY * GZ, GZ, 1)
     coords = (space_pos // (GY * GZ), space_pos // GZ % GY, space_pos % GZ)

time: 272 us -> 319 us (1.17)
  starting transfers between devices: 27.3 us -> 77.1 us
  matrix products: 22.9 us -> 14.5 us
    ppermute x0 -> x7, waiting for transfers between devices: none -> 75.6 us  [boxes_supply_all(): ppermute(bank[j0 - 1], 'space', [(i0, (i0 - 1) % n_parts) for i0 in range...]
    all_gather x1 -> x0, waiting for transfers between devices: 73.2 us -> none  [shards(): lax.all_gather(new_master.astype(jnp.bfloat16), 'space', axis=1, tiled=True)]
    ppermute x0 -> x7, starting transfers between devices: none -> 49.2 us  [boxes_supply_all(): ppermute(bank[j0 - 1], 'space', [(i0, (i0 - 1) % n_parts) for i0 in range...]
    dot_general x54, matrix products: 22.9 us -> 14.5 us  [convolve(): jnp.dot(window.reshape(-1, channels), weights_tap, preferred_element_type...]
    unnamed x42 -> x25, local copies, waits for them, and re-layouts: 6.87 us -> 12.2 us
  transfers between devices with their start and end apart: 15 -> 21, of which waited for: 13 -> 14; matrix products, arithmetic and copies ran while one was open for 3% -> 3% of each run, Pallas kernels for 0% -> 0%
where the time goes in v1:
time: 319 us; the launch traced here: 317 us
  waiting for transfers between devices  178 us (56%)
  starting transfers between devices  77.1 us (24%)
  between operations  20.1 us (6%)
  local copies, waits for them, and re-layouts  15.9 us (5%)
  matrix products  14.5 us (5%)
  other arithmetic  11.7 us (4%)
    ppermute x7, waiting for transfers between devices, boxes_supply_all(): ppermute(bank[j0 - 1], 'space', [(i0, (i0 - 1) % n_parts) for i0 in range...  75.6 us
    ppermute x7, starting transfers between devices, boxes_supply_all(): ppermute(bank[j0 - 1], 'space', [(i0, (i0 - 1) % n_parts) for i0 in range...  49.2 us
    psum x1, waiting for transfers between devices, spread(): return lax.psum(kept, axis)  36.1 us
    psum x1, waiting for transfers between devices, shards(): lax.psum(grad_parts[0].astype(jnp.float32).astype(jnp.bfloat16), 'rep')  34 us
    ppermute x12, waiting for transfers between devices, passed_along(): lax.ppermute(value, axis, [(source, source + steps) for source in range(f...  31.4 us
    ppermute x12, starting transfers between devices, passed_along(): lax.ppermute(value, axis, [(source, source + steps) for source in range(f...  27.8 us
    dot_general x54, matrix products, convolve(): jnp.dot(window.reshape(-1, channels), weights_tap, preferred_element_type...  14.5 us
    unnamed x25, local copies, waits for them, and re-layouts  12.2 us
  transfers between devices with their start and end apart: 21, of which 14 were waited for; matrix products, arithmetic and copies ran while one was open for 3% of the time, Pallas kernels for 0%

profile of v1, /device:TPU:0, one launch (start us, length us, event | category | flops | bytes accessed | tf_op | source)
XLA Modules:
  0.0 317.0 jit_solution(13571468652632524587)
XLA Ops:
  14.7 34.0 %all-reduce.4.cloned.1.call-done = bf16[2,864,256]{2,1,0:T(8,128)(2,1)} async-done(((bf16[2,864,256]{2,1,0:T(8,128)(2,1)}), bf16[2,864,256]{2,1,0:T(8,128)(2,1)}) %all-reduce.4.cloned.1.call-update) | async-done | bytes 884752 | tf_op jit(solution)/shard_map/psum | solution.py:90
  48.7 4.8 %fusion.8 = (f32[1,2,864,256]{3,2,1,0:T(8,128)}, bf16[2,864,256]{2,1,0:T(8,128)(2,1)S(1)}, f32[1,2,864,256]{3,2,1,0:T(8,128)}) fusion(bf16[2,864,256]{2,1,0:T(8,128)(2,1)} %all-reduce.4.cloned.1.call-done, f32[1,2,864,256]{3,2,1,0:T(8,128)} %param.10, pred[2,864]{1,0:T(4,128)(4,1)S(1)} %eq.54, f32[2,864,256]{2,1,0:T(8,128)} %param.8, f32[1,2,864,256]{3,2,1,0:T(8,128)} %param.9), kind=kLoop, calls=%fused_computation.12 | loop fusion | flops 8404992 | bytes 10618560 | tf_op jit(solution)/shard_map/broadcast_in_dim | solution.py:99
  54.5 36.1 %all-reduce.6.cloned.1.call-done = (bf16[216,256]{1,0:T(8,128)(2,1)}, bf16[216,256]{1,0:T(8,128)(2,1)}, bf16[216,256]{1,0:T(8,128)(2,1)}, bf16[216,256]{1,0:T(8,...) async-done(((bf16[216,256]{1,0:T(8,128)(2,1)}, bf16[216,256]{1,0:T(8,128)(2,1)}, ...) | async-done | bytes 884752 | tf_op jit(solution)/shard_map/psum | solution.py:32
  98.1 4.2 %collective-permute-start.5 = (bf16[2,864,256]{2,1,0:T(8,128)(2,1)S(1)}, bf16[2,864,256]{2,1,0:T(8,128)(2,1)S(1)}, u32[]{:S(2)}, u32[]{:S(2)}) collective-permute-start(bf16[2,864,256]{2,1,0:T(8,128)(2,1)S(1)} %get-tuple-element.17), channel_id=1, source_target_pairs={{0,28},{4,0},{8,4},{12,8},{16,12},{20,16},{24,20},{28,24},{1,29},{... | collective-permute-start | bytes 2654216 | tf_op jit(solution)/shard_map/ppermute | solution.py:17
  102.3 18.0 %collective-permute-done.5 = bf16[2,864,256]{2,1,0:T(8,128)(2,1)S(1)} collective-permute-done((bf16[2,864,256]{2,1,0:T(8,128)(2,1)S(1)}, bf16[2,864,256]{2,1,0:T(8,128)(2,1)S(1)}, u32[]{:S(2)}, u32[]{:S(2)}) %collective-permute-start.5) | collective-permute-done | bytes 884768 | tf_op jit(solution)/shard_map/ppermute | solution.py:17
  120.2 5.2 %collective-permute-start.6 = (bf16[2,864,256]{2,1,0:T(8,128)(2,1)S(1)}, bf16[2,864,256]{2,1,0:T(8,128)(2,1)S(1)}, u32[]{:S(2)}, u32[]{:S(2)}) collective-permute-start(bf16[2,864,256]{2,1,0:T(8,128)(2,1)S(1)} %collective-permute-done.5), channel_id=1, source_target_pairs={{0,28},{4,0},{8,4},{12,8},{16,12},{20,16},{24,20},{28,24},{1,29},{... | collective-permute-start | bytes 2654216 | tf_op jit(solution)/shard_map/ppermute | solution.py:17
  125.4 17.1 %collective-permute-done.6 = bf16[2,864,256]{2,1,0:T(8,128)(2,1)S(1)} collective-permute-done((bf16[2,864,256]{2,1,0:T(8,128)(2,1)S(1)}, bf16[2,864,256]{2,1,0:T(8,128)(2,1)S(1)}, u32[]{:S(2)}, u32[]{:S(2)}) %collective-permute-start.6) | collective-permute-done | bytes 884768 | tf_op jit(solution)/shard_map/ppermute | solution.py:17
  142.5 5.2 %collective-permute-start.7 = (bf16[2,864,256]{2,1,0:T(8,128)(2,1)S(1)}, bf16[2,864,256]{2,1,0:T(8,128)(2,1)}, u32[]{:S(2)}, u32[]{:S(2)}) collective-permute-start(bf16[2,864,256]{2,1,0:T(8,128)(2,1)S(1)} %collective-permute-done.6), channel_id=1, source_target_pairs={{0,28},{4,0},{8,4},{12,8},{16,12},{20,16},{24,20},{28,24},{1,29},{... | collective-permute-start | bytes 2654216 | tf_op jit(solution)/shard_map/ppermute | solution.py:17
  147.7 16.2 %collective-permute-done.7 = bf16[2,864,256]{2,1,0:T(8,128)(2,1)} collective-permute-done((bf16[2,864,256]{2,1,0:T(8,128)(2,1)S(1)}, bf16[2,864,256]{2,1,0:T(8,128)(2,1)}, u32[]{:S(2)}, u32[]{:S(2)}) %collective-permute-start.7) | collective-permute-done | bytes 884768 | tf_op jit(solution)/shard_map/ppermute | solution.py:17
  164.0 5.4 %collective-permute-start.8 = (bf16[2,864,256]{2,1,0:T(8,128)(2,1)}, bf16[2,864,256]{2,1,0:T(8,128)(2,1)}, u32[]{:S(2)}, u32[]{:S(2)}) collective-permute-start(bf16[2,864,256]{2,1,0:T(8,128)(2,1)} %collective-permute-done.7), channel_id=1, source_target_pairs={{0,28},{4,0},{8,4},{12,8},{16,12},{20,16},{24,20},{28,24},{1,29},{... | collective-permute-start | bytes 2654216 | tf_op jit(solution)/shard_map/ppermute | solution.py:17
  172.0 15.0 %collective-permute-done = bf16[1,4,16,256]{3,2,1,0:T(8,128)(2,1)S(1)} collective-permute-done((bf16[1,4,16,256]{3,2,1,0:T(8,128)(2,1)S(1)}, bf16[1,4,16,256]{3,2,1,0:T(8,128)(2,1)S(1)}, u32[]{:S(2)}, u32[]{:S(2)}) %collective-permute-start) | collective-permute-done | bytes 32800 | tf_op jit(solution)/shard_map/ppermute | solution.py:27
  189.7 2.0 collective-permute-start.9
  191.7 6.5 %collective-permute-done.3 = bf16[10,1,16,256]{3,2,1,0:T(8,128)(2,1)S(1)} collective-permute-done((bf16[10,1,16,256]{3,2,1,0:T(8,128)(2,1)S(1)}, bf16[10,1,16,256]{3,2,1,0:T(8,128)(2,1)S(1)}, u32[]{:S(2)}, u32[]{:S(2)}) %collective-permute-start.3) | collective-permute-done | bytes 81952 | tf_op jit(solution)/shard_map/ppermute | solution.py:27
  199.6 4.5 %collective-permute-start.4 = (bf16[10,6,1,256]{3,2,1,0:T(2,128)(2,1)S(1)}, bf16[10,6,1,256]{3,2,1,0:T(2,128)(2,1)S(1)}, u32[]{:S(2)}, u32[]{:S(2)}) collective-permute-start(bf16[10,6,1,256]{3,2,1,0:T(2,128)(2,1)S(1)} %get-tuple-element.69), channel_id=1, source_target_pairs={{0,4},{4,8},{8,12},{12,16},{16,20},{20,24},{24,28},{1,5},{5,9},{9,... | collective-permute-start | bytes 92168 | tf_op jit(solution)/shard_map/ppermute | solution.py:27
  204.4 2.9 collective-permute-done.9
  207.4 18.7 %collective-permute-start.10 = (bf16[2,864,256]{2,1,0:T(8,128)(2,1)S(1)}, bf16[2,864,256]{2,1,0:T(8,128)(2,1)S(1)}, u32[]{:S(2)}, u32[]{:S(2)}) collective-permute-start(bf16[2,864,256]{2,1,0:T(8,128)(2,1)S(1)} %collective-permute-done.9), channel_id=1, source_target_pairs={{0,28},{4,0},{8,4},{12,8},{16,12},{20,16},{24,20},{28,24},{1,29},{... | collective-permute-start | bytes 2654216 | tf_op jit(solution)/shard_map/ppermute | solution.py:17
  228.9 14.4 %collective-permute-done.10 = bf16[2,864,256]{2,1,0:T(8,128)(2,1)S(1)} collective-permute-done((bf16[2,864,256]{2,1,0:T(8,128)(2,1)S(1)}, bf16[2,864,256]{2,1,0:T(8,128)(2,1)S(1)}, u32[]{:S(2)}, u32[]{:S(2)}) %collective-permute-start.10) | collective-permute-done | bytes 884768 | tf_op jit(solution)/shard_map/ppermute | solution.py:17
  243.3 8.6 %collective-permute-start.11 = (bf16[2,864,256]{2,1,0:T(8,128)(2,1)S(1)}, bf16[2,864,256]{2,1,0:T(8,128)(2,1)S(1)}, u32[]{:S(2)}, u32[]{:S(2)}) collective-permute-start(bf16[2,864,256]{2,1,0:T(8,128)(2,1)S(1)} %collective-permute-done.10), channel_id=1, source_target_pairs={{0,28},{4,0},{8,4},{12,8},{16,12},{20,16},{24,20},{28,24},{1,29},{... | collective-permute-start | bytes 2654216 | tf_op jit(solution)/shard_map/ppermute | solution.py:17
  255.9 6.9 %collective-permute-done.11 = bf16[2,864,256]{2,1,0:T(8,128)(2,1)S(1)} collective-permute-done((bf16[2,864,256]{2,1,0:T(8,128)(2,1)S(1)}, bf16[2,864,256]{2,1,0:T(8,128)(2,1)S(1)}, u32[]{:S(2)}, u32[]{:S(2)}) %collective-permute-start.11) | collective-permute-done | bytes 884768 | tf_op jit(solution)/shard_map/ppermute | solution.py:17
  273.3 2.1 collective-permute-start.13
  277.0 5.1 %collective-permute-done.14 = bf16[1,4,16,256]{3,2,1,0:T(8,128)(2,1)S(1)} collective-permute-done((bf16[1,4,16,256]{3,2,1,0:T(8,128)(2,1)S(1)}, bf16[1,4,16,256]{3,2,1,0:T(8,128)(2,1)S(1)}, u32[]{:S(2)}, u32[]{:S(2)}) %collective-permute-start.14) | collective-permute-done | bytes 32800 | tf_op jit(solution)/shard_map/ppermute | solution.py:27
  282.2 3.3 %collective-permute-start.15 = (bf16[10,1,16,256]{3,2,1,0:T(8,128)(2,1)S(1)}, bf16[10,1,16,256]{3,2,1,0:T(8,128)(2,1)S(1)}, u32[]{:S(2)}, u32[]{:S(2)}) collective-permute-start(bf16[10,1,16,256]{3,2,1,0:T(8,128)(2,1)S(1)} %get-tuple-element.85), channel_id=1, source_target_pairs={{0,8},{4,12},{8,16},{12,20},{16,24},{20,28},{1,9},{5,13},{9,17},{1... | collective-permute-start | bytes 245768 | tf_op jit(solution)/shard_map/ppermute | solution.py:27
  287.5 4.3 %collective-permute-done.16 = bf16[10,1,16,256]{3,2,1,0:T(8,128)(2,1)S(1)} collective-permute-done((bf16[10,1,16,256]{3,2,1,0:T(8,128)(2,1)S(1)}, bf16[10,1,16,256]{3,2,1,0:T(8,128)(2,1)S(1)}, u32[]{:S(2)}, u32[]{:S(2)}) %collective-permute-start.16) | collective-permute-done | bytes 81952 | tf_op jit(solution)/shard_map/ppermute | solution.py:27
  293.6 7.4 %collective-permute-start.17 = (bf16[10,6,1,256]{3,2,1,0:T(2,128)(2,1)S(1)}, bf16[10,6,1,256]{3,2,1,0:T(2,128)(2,1)S(1)}, u32[]{:S(2)}, u32[]{:S(2)}) collective-permute-start(bf16[10,6,1,256]{3,2,1,0:T(2,128)(2,1)S(1)} %get-tuple-element.65), channel_id=1, source_target_pairs={{0,4},{4,8},{8,12},{12,16},{16,20},{20,24},{24,28},{1,5},{5,9},{9,... | collective-permute-start | bytes 92168 | tf_op jit(solution)/shard_map/ppermute | solution.py:27
  (142 shorter events, 49.1 us)
Async XLA Ops:
  7.2 162.2 %copy-start = (bf16[1,1,8,4,16,256]{5,4,3,2,1,0:T(8,128)(2,1)S(1)}, bf16[1,1,8,4,16,256]{5,4,3,2,1,0:T(8,128)(2,1)}, u32[]{:S(2)}) copy-start(bf16[1,1,8,4,16,256]{5,4,3,2,1,0:T(8,128)(2,1)} %param.6) | copy-start | bytes 786436
  7.2 41.6 %all-reduce.4.cloned.1.call-start = ((), (), s32[]{:S(2)}) async-start(), calls=%async_computation | async-start | bytes 1769472 | tf_op jit(solution)/shard_map/psum | solution.py:90
  7.9 82.7 %all-reduce.6.cloned.1.call-start = ((), (), s32[]{:S(2)}) async-start(), calls=%async_computation.1 | async-start | bytes 1769472 | tf_op jit(solution)/shard_map/psum | solution.py:32
  98.1 22.2 %collective-permute-start.5 = (bf16[2,864,256]{2,1,0:T(8,128)(2,1)S(1)}, bf16[2,864,256]{2,1,0:T(8,128)(2,1)S(1)}, u32[]{:S(2)}, u32[]{:S(2)}) collective-permute-start(bf16[2,864,256]{2,1,0:T(8,128)(2,1)S(1)} %get-tuple-element.17), channel_id=1, source_target_pairs={{0,28},{4,0},{8,4},{12,8},{16,12},{20,16},{24,20},{28,24},{1,29},{... | collective-permute-start | bytes 2654216 | tf_op jit(solution)/shard_map/ppermute | solution.py:17
  120.2 22.3 %collective-permute-start.6 = (bf16[2,864,256]{2,1,0:T(8,128)(2,1)S(1)}, bf16[2,864,256]{2,1,0:T(8,128)(2,1)S(1)}, u32[]{:S(2)}, u32[]{:S(2)}) collective-permute-start(bf16[2,864,256]{2,1,0:T(8,128)(2,1)S(1)} %collective-permute-done.5), channel_id=1, source_target_pairs={{0,28},{4,0},{8,4},{12,8},{16,12},{20,16},{24,20},{28,24},{1,29},{... | collective-permute-start | bytes 2654216 | tf_op jit(solution)/shard_map/ppermute | solution.py:17
  142.5 21.4 %collective-permute-start.7 = (bf16[2,864,256]{2,1,0:T(8,128)(2,1)S(1)}, bf16[2,864,256]{2,1,0:T(8,128)(2,1)}, u32[]{:S(2)}, u32[]{:S(2)}) collective-permute-start(bf16[2,864,256]{2,1,0:T(8,128)(2,1)S(1)} %collective-permute-done.6), channel_id=1, source_target_pairs={{0,28},{4,0},{8,4},{12,8},{16,12},{20,16},{24,20},{28,24},{1,29},{... | collective-permute-start | bytes 2654216 | tf_op jit(solution)/shard_map/ppermute | solution.py:17
  164.0 25.8 %collective-permute-start.8 = (bf16[2,864,256]{2,1,0:T(8,128)(2,1)}, bf16[2,864,256]{2,1,0:T(8,128)(2,1)}, u32[]{:S(2)}, u32[]{:S(2)}) collective-permute-start(bf16[2,864,256]{2,1,0:T(8,128)(2,1)} %collective-permute-done.7), channel_id=1, source_target_pairs={{0,28},{4,0},{8,4},{12,8},{16,12},{20,16},{24,20},{28,24},{1,29},{... | collective-permute-start | bytes 2654216 | tf_op jit(solution)/shard_map/ppermute | solution.py:17
  169.3 17.7 %collective-permute-start = (bf16[1,4,16,256]{3,2,1,0:T(8,128)(2,1)S(1)}, bf16[1,4,16,256]{3,2,1,0:T(8,128)(2,1)S(1)}, u32[]{:S(2)}, u32[]{:S(2)}) collective-permute-start(bf16[1,4,16,256]{3,2,1,0:T(8,128)(2,1)S(1)} %get-tuple-element.97), channel_id=1, source_target_pairs={{0,16},{4,20},{8,24},{12,28},{1,17},{5,21},{9,25},{13,29},{2,18},{... | collective-permute-start | bytes 98312 | tf_op jit(solution)/shard_map/ppermute | solution.py:27
  170.6 16.4 %collective-permute-start.1 = (bf16[1,4,16,256]{3,2,1,0:T(8,128)(2,1)S(1)}, bf16[1,4,16,256]{3,2,1,0:T(8,128)(2,1)S(1)}, u32[]{:S(2)}, u32[]{:S(2)}) collective-permute-start(bf16[1,4,16,256]{3,2,1,0:T(8,128)(2,1)S(1)} %get-tuple-element.98), channel_id=1, source_target_pairs={{16,0},{20,4},{24,8},{28,12},{17,1},{21,5},{25,9},{29,13},{18,2},{... | collective-permute-start | bytes 98312 | tf_op jit(solution)/shard_map/ppermute | solution.py:27
  172.0 81.2 %copy-start.1 = (bf16[2,13824,256]{2,1,0:T(8,128)(2,1)S(1)}, bf16[2,13824,256]{2,1,0:T(8,128)(2,1)}, u32[]{:S(2)}) copy-start(bf16[2,13824,256]{2,1,0:T(8,128)(2,1)} %get-tuple-element.18) | copy-start | bytes 42467332
  187.1 4.6 %collective-permute-start.2 = (bf16[10,1,16,256]{3,2,1,0:T(8,128)(2,1)S(1)}, bf16[10,1,16,256]{3,2,1,0:T(8,128)(2,1)S(1)}, u32[]{:S(2)}, u32[]{:S(2)}) collective-permute-start(bf16[10,1,16,256]{3,2,1,0:T(8,128)(2,1)S(1)} %get-tuple-element.89), channel_id=1, source_target_pairs={{0,8},{4,12},{8,16},{12,20},{16,24},{20,28},{1,9},{5,13},{9,17},{1... | collective-permute-start | bytes 245768 | tf_op jit(solution)/shard_map/ppermute | solution.py:27
  188.4 9.8 %collective-permute-start.3 = (bf16[10,1,16,256]{3,2,1,0:T(8,128)(2,1)S(1)}, bf16[10,1,16,256]{3,2,1,0:T(8,128)(2,1)S(1)}, u32[]{:S(2)}, u32[]{:S(2)}) collective-permute-start(bf16[10,1,16,256]{3,2,1,0:T(8,128)(2,1)S(1)} %get-tuple-element.90), channel_id=1, source_target_pairs={{8,0},{12,4},{16,8},{20,12},{24,16},{28,20},{9,1},{13,5},{17,9},{2... | collective-permute-start | bytes 245768 | tf_op jit(solution)/shard_map/ppermute | solution.py:27
  189.7 17.6 %collective-permute-start.9 = (bf16[2,864,256]{2,1,0:T(8,128)(2,1)}, bf16[2,864,256]{2,1,0:T(8,128)(2,1)S(1)}, u32[]{:S(2)}, u32[]{:S(2)}) collective-permute-start(bf16[2,864,256]{2,1,0:T(8,128)(2,1)} %collective-permute-done.8), channel_id=1, source_target_pairs={{0,28},{4,0},{8,4},{12,8},{16,12},{20,16},{24,20},{28,24},{1,29},{... | collective-permute-start | bytes 2654216 | tf_op jit(solution)/shard_map/ppermute | solution.py:17
  198.3 27.8 %collective-permute-start.12 = (bf16[10,6,1,256]{3,2,1,0:T(2,128)(2,1)S(1)}, bf16[10,6,1,256]{3,2,1,0:T(2,128)(2,1)S(1)}, u32[]{:S(2)}, u32[]{:S(2)}) collective-permute-start(bf16[10,6,1,256]{3,2,1,0:T(2,128)(2,1)S(1)} %get-tuple-element.70), channel_id=1, source_target_pairs={{4,0},{8,4},{12,8},{16,12},{20,16},{24,20},{28,24},{5,1},{9,5},{13... | collective-permute-start | bytes 92168 | tf_op jit(solution)/shard_map/ppermute | solution.py:27
  199.6 26.5 %collective-permute-start.4 = (bf16[10,6,1,256]{3,2,1,0:T(2,128)(2,1)S(1)}, bf16[10,6,1,256]{3,2,1,0:T(2,128)(2,1)S(1)}, u32[]{:S(2)}, u32[]{:S(2)}) collective-permute-start(bf16[10,6,1,256]{3,2,1,0:T(2,128)(2,1)S(1)} %get-tuple-element.69), channel_id=1, source_target_pairs={{0,4},{4,8},{8,12},{12,16},{16,20},{20,24},{24,28},{1,5},{5,9},{9,... | collective-permute-start | bytes 92168 | tf_op jit(solution)/shard_map/ppermute | solution.py:27
  207.4 35.9 %collective-permute-start.10 = (bf16[2,864,256]{2,1,0:T(8,128)(2,1)S(1)}, bf16[2,864,256]{2,1,0:T(8,128)(2,1)S(1)}, u32[]{:S(2)}, u32[]{:S(2)}) collective-permute-start(bf16[2,864,256]{2,1,0:T(8,128)(2,1)S(1)} %collective-permute-done.9), channel_id=1, source_target_pairs={{0,28},{4,0},{8,4},{12,8},{16,12},{20,16},{24,20},{28,24},{1,29},{... | collective-permute-start | bytes 2654216 | tf_op jit(solution)/shard_map/ppermute | solution.py:17
  243.3 19.6 %collective-permute-start.11 = (bf16[2,864,256]{2,1,0:T(8,128)(2,1)S(1)}, bf16[2,864,256]{2,1,0:T(8,128)(2,1)S(1)}, u32[]{:S(2)}, u32[]{:S(2)}) collective-permute-start(bf16[2,864,256]{2,1,0:T(8,128)(2,1)S(1)} %collective-permute-done.10), channel_id=1, source_target_pairs={{0,28},{4,0},{8,4},{12,8},{16,12},{20,16},{24,20},{28,24},{1,29},{... | collective-permute-start | bytes 2654216 | tf_op jit(solution)/shard_map/ppermute | solution.py:17
  273.3 3.7 %collective-permute-start.13 = (bf16[1,4,16,256]{3,2,1,0:T(8,128)(2,1)S(1)}, bf16[1,4,16,256]{3,2,1,0:T(8,128)(2,1)S(1)}, u32[]{:S(2)}, u32[]{:S(2)}) collective-permute-start(bf16[1,4,16,256]{3,2,1,0:T(8,128)(2,1)S(1)} %get-tuple-element.93), channel_id=1, source_target_pairs={{0,16},{4,20},{8,24},{12,28},{1,17},{5,21},{9,25},{13,29},{2,18},{... | collective-permute-start | bytes 98312 | tf_op jit(solution)/shard_map/ppermute | solution.py:27
  275.4 6.7 %collective-permute-start.14 = (bf16[1,4,16,256]{3,2,1,0:T(8,128)(2,1)S(1)}, bf16[1,4,16,256]{3,2,1,0:T(8,128)(2,1)S(1)}, u32[]{:S(2)}, u32[]{:S(2)}) collective-permute-start(bf16[1,4,16,256]{3,2,1,0:T(8,128)(2,1)S(1)} %get-tuple-element.94), channel_id=1, source_target_pairs={{16,0},{20,4},{24,8},{28,12},{17,1},{21,5},{25,9},{29,13},{18,2},{... | collective-permute-start | bytes 98312 | tf_op jit(solution)/shard_map/ppermute | solution.py:27
  282.2 5.3 %collective-permute-start.15 = (bf16[10,1,16,256]{3,2,1,0:T(8,128)(2,1)S(1)}, bf16[10,1,16,256]{3,2,1,0:T(8,128)(2,1)S(1)}, u32[]{:S(2)}, u32[]{:S(2)}) collective-permute-start(bf16[10,1,16,256]{3,2,1,0:T(8,128)(2,1)S(1)} %get-tuple-element.85), channel_id=1, source_target_pairs={{0,8},{4,12},{8,16},{12,20},{16,24},{20,28},{1,9},{5,13},{9,17},{1... | collective-permute-start | bytes 245768 | tf_op jit(solution)/shard_map/ppermute | solution.py:27
  285.4 6.3 %collective-permute-start.16 = (bf16[10,1,16,256]{3,2,1,0:T(8,128)(2,1)S(1)}, bf16[10,1,16,256]{3,2,1,0:T(8,128)(2,1)S(1)}, u32[]{:S(2)}, u32[]{:S(2)}) collective-permute-start(bf16[10,1,16,256]{3,2,1,0:T(8,128)(2,1)S(1)} %get-tuple-element.86), channel_id=1, source_target_pairs={{8,0},{12,4},{16,8},{20,12},{24,16},{28,20},{9,1},{13,5},{17,9},{2... | collective-permute-start | bytes 245768 | tf_op jit(solution)/shard_map/ppermute | solution.py:27
  292.3 10.0 %collective-permute-start.18 = (bf16[10,6,1,256]{3,2,1,0:T(2,128)(2,1)S(1)}, bf16[10,6,1,256]{3,2,1,0:T(2,128)(2,1)S(1)}, u32[]{:S(2)}, u32[]{:S(2)}) collective-permute-start(bf16[10,6,1,256]{3,2,1,0:T(2,128)(2,1)S(1)} %get-tuple-element.66), channel_id=1, source_target_pairs={{4,0},{8,4},{12,8},{16,12},{20,16},{24,20},{28,24},{5,1},{9,5},{13... | collective-permute-start | bytes 92168 | tf_op jit(solution)/shard_map/ppermute | solution.py:27
  293.6 9.2 %collective-permute-start.17 = (bf16[10,6,1,256]{3,2,1,0:T(2,128)(2,1)S(1)}, bf16[10,6,1,256]{3,2,1,0:T(2,128)(2,1)S(1)}, u32[]{:S(2)}, u32[]{:S(2)}) collective-permute-start(bf16[10,6,1,256]{3,2,1,0:T(2,128)(2,1)S(1)} %get-tuple-element.65), channel_id=1, source_target_pairs={{0,4},{4,8},{8,12},{12,16},{16,20},{20,24},{24,28},{1,5},{5,9},{9,... | collective-permute-start | bytes 92168 | tf_op jit(solution)/shard_map/ppermute | solution.py:27
Sparse Core Ops, SparseCore 0:
  10.4 38.3 all-reduce.3
  54.6 35.9 all-reduce.5
